TPU v7x, 32 devices: a whole 2x2x4 slice. The times are simulated.
32 devices in a mesh: dp: 4 (over y, x), fsdp: 8 (over z, core).
Axes of the slice: x: 2, y: 2, z: 4, core: 2. Of those that a mesh axis runs over, the one named last changes fastest.
Arguments:
- hidden: bfloat16 [2, 4608, 4096], P(None, ('dp', 'fsdp')), may hold values from -120 to 120
- cotangent: bfloat16 [2, 4608, 1024], P(None, ('dp', 'fsdp')), may hold values from -6 to 6
- proj_weight: bfloat16 [2, 4096, 1024], P(None, 'fsdp'), may hold values from -3 to 3
- norm_gain: float32 [2, 4096], replicated, may hold values from 0.1 to 1.9
- prev_factor: bfloat16 [2, 512, 128], replicated, may hold values from -0.25 to 0.25
- factor_ranks: int32 [2, 2], replicated, may hold values from 4 to 64, as said below
- layer_order: int32 [2], replicated, may hold values from 0 to 1, each once
Outputs:
- hidden_grad: bfloat16 [4608, 4096], P(('dp', 'fsdp'))
- basis_factor: float32 [2, 4096, 128], P(None, 'fsdp')
Inputs may be any that keep to these rules, and one draw needn't show every extreme that they name: `factor_ranks`: every draw holds a rank equal to 64 and a rank equal to 4.
All inputs are finite; a program needn't handle non-finite values.
Results may differ from a plain program's by a relative error of at most 0.0056.
Values may be sent and summed in bfloat16 or wider, within the bound.
A program may use at most 64 MiB of HBM per device.

v0:
```python
import math

import jax
import jax.numpy as jnp
from jax import lax
from jax.sharding import PartitionSpec as P

D = 4096


def normalize(hidden_rows, gain_row):
    wide_rows = hidden_rows.astype(jnp.float32)
    inverse = lax.rsqrt(jnp.mean(wide_rows * wide_rows, axis=1, keepdims=True) + 1e-05)
    normed = (wide_rows * inverse * gain_row[None, :]).astype(jnp.bfloat16)
    return (inverse, normed)


def masked_factors(factors, rank_pair):
    rank_cols = factors.shape[1] // 2
    position = jnp.arange(2 * rank_cols)
    column = position % rank_cols
    column_limit = jnp.where(position < rank_cols, rank_pair[0], rank_pair[1])
    return jnp.where((column < column_limit)[None, :], factors, jnp.zeros_like(factors))


def project(grad_rows, kept_factor):
    head_cols = grad_rows.shape[1] // 2
    rank_cols = kept_factor.shape[1] // 2
    keys_part = jnp.dot(
        grad_rows[:, :head_cols], kept_factor[:, :rank_cols], preferred_element_type=jnp.float32
    )
    values_part = jnp.dot(
        grad_rows[:, head_cols:], kept_factor[:, rank_cols:], preferred_element_type=jnp.float32
    )
    return jnp.concatenate([keys_part, values_part], axis=1).astype(jnp.bfloat16)


def gram_pair(factor_shard):
    row_count = factor_shard.shape[0]
    rank_cols = factor_shard.shape[1] // 2
    paired = factor_shard.reshape(row_count, 2, rank_cols)
    return jnp.einsum(
        "rmi,rmj->mij",
        paired,
        paired,
        precision=lax.Precision.HIGHEST,
        preferred_element_type=jnp.float32,
    )


def orthonormal(factor_shard, gram_totals, rank_pair):
    rank_cols = factor_shard.shape[1] // 2
    column = jnp.arange(rank_cols)
    pieces = []
    for member in range(2):
        block_cols = factor_shard[:, member * rank_cols : (member + 1) * rank_cols]
        padded = gram_totals[member] + jnp.diag((column >= rank_pair[member]).astype(jnp.float32))
        lower_factor = jnp.linalg.cholesky(padded)
        pieces.append(
            lax.linalg.triangular_solve(
                lower_factor, block_cols, left_side=False, lower=True, transpose_a=True
            )
        )
    return math.sqrt(D) * jnp.concatenate(pieces, axis=1)


def body(hidden, cotangent, proj_weight, norm_gain, prev_factor, factor_ranks, layer_order):
    layer_count = hidden.shape[0]
    top_slot = layer_order[0]
    inverses = []
    shards = []
    basis_list = []
    for slot_index in range(layer_count):
        inverse, normed = normalize(hidden[slot_index], norm_gain[slot_index])
        inverses.append(inverse)
        kept_factor = masked_factors(prev_factor[slot_index], factor_ranks[slot_index])
        projected = project(cotangent[slot_index], kept_factor)
        local_rows = lax.psum_scatter(
            lax.dot_general(
                normed, projected, (((0,), (0,)), ((), ())), preferred_element_type=jnp.float32
            ),
            "fsdp",
            scatter_dimension=0,
            tiled=True,
        )
        factor_shard = lax.psum(local_rows, "dp")
        shards.append(factor_shard)
    stacked = jnp.stack([gram_pair(factor_shard) for factor_shard in shards])
    all_grams = lax.psum(stacked, "fsdp")
    basis_list = [
        orthonormal(shards[slot_index], all_grams[slot_index], factor_ranks[slot_index])
        for slot_index in range(layer_count)
    ]
    top_grads = lax.dynamic_index_in_dim(cotangent, top_slot, 0, keepdims=False)
    top_weight = lax.dynamic_index_in_dim(proj_weight, top_slot, 0, keepdims=False)
    input_grad = lax.dot_general(
        top_grads,
        lax.all_gather(top_weight, "fsdp", axis=0, tiled=True),
        (((1,), (1,)), ((), ())),
        preferred_element_type=jnp.float32,
    )
    top_inverse = lax.dynamic_index_in_dim(jnp.stack(inverses), top_slot, 0, keepdims=False)
    top_gain = lax.dynamic_index_in_dim(norm_gain, top_slot, 0, keepdims=False)
    top_hidden = lax.dynamic_index_in_dim(hidden, top_slot, 0, keepdims=False).astype(jnp.float32)
    scaled = input_grad * top_gain[None, :]
    unit_rows = top_hidden * top_inverse
    inner_mean = jnp.mean(scaled * unit_rows, axis=1, keepdims=True)
    hidden_grad = (top_inverse * (scaled - unit_rows * inner_mean)).astype(jnp.bfloat16)
    return (hidden_grad, jnp.stack(basis_list))


def solution(mesh):
    in_specs = (
        P(None, ("dp", "fsdp"), None),
        P(None, ("dp", "fsdp"), None),
        P(None, "fsdp", None),
        P(),
        P(),
        P(),
        P(),
    )
    out_specs = (P(("dp", "fsdp"), None), P(None, "fsdp", None))
    return jax.shard_map(body, mesh=mesh, in_specs=in_specs, out_specs=out_specs, check_vma=False)
```

profile of v0, /device:TPU:0, one launch (start us, length us, event | category | flops | bytes accessed | tf_op | source)
XLA Modules:
  0.0 299.6 jit_solution(16446004569142756650)
XLA Ops:
  7.2 1.2 slice_bitcast_fusion.1
  8.5 1.4 fusion.76
  9.9 2.4 fusion.71
  12.3 1.0 bitcast_select_fusion.1
  13.3 0.3 fusion.30
  13.6 0.2 fusion.29
  13.9 2.2 fusion.8
  16.2 3.5 %fusion.17 = f32[4096,128]{1,0:T(8,128)} fusion(f32[4096]{0:T(1024)S(1)} %bitcast.139, f32[144]{0:T(256)S(1)} %add_rsqrt_fusion, bf16[2,144,4096]{2,1,0:T(8,128)(2,1)} %param.10, bf16[144,64]{0,1:T(8,128)(2,1)S(1)} %fusion.30, bf16[144,64]{0,1:T(8,128)(2,1)S(1)} %fusion.29), kind=kOutput, calls=%fused_computation.20 | convolution fusion | flops 153427968 | bytes 3330624 | tf_op jit(solution)/shard_map/dot_general | solution.py:79
  19.8 0.3 fusion.28
  20.3 3.5 %fusion.19 = f32[4096,128]{1,0:T(8,128)} fusion(f32[4096]{0:T(1024)S(1)} %bitcast.138, f32[144]{0:T(256)S(1)} %add_rsqrt_fusion.1, bf16[2,144,4096]{2,1,0:T(8,128)(2,1)} %param.10, bf16[144,64]{0,1:T(8,128)(2,1)S(1)} %fusion.28, bf16[144,64]{0,1:T(8,128)(2,1)S(1)} %fusion.27), kind=kOutput, calls=%fused_computation.21 | convolution fusion | flops 153427968 | bytes 3330624 | tf_op jit(solution)/shard_map/dot_general | solution.py:79
  23.8 34.8 %reduce-scatter.5.cloned.1.call-done = f32[512,128]{1,0:T(8,128)} async-done(((f32[4096,128]{1,0:T(8,128)}), f32[512,128]{1,0:T(8,128)}) %reduce-scatter.5.cloned.1.call-update) | async-done | bytes 262160 | tf_op jit(solution)/shard_map/reduce_scatter | solution.py:78
  58.6 37.0 %reduce-scatter.3.cloned.1.call-done = f32[512,128]{1,0:T(8,128)} async-done(((f32[4096,128]{1,0:T(8,128)}), f32[512,128]{1,0:T(8,128)}) %reduce-scatter.3.cloned.1.call-update) | async-done | bytes 262160 | tf_op jit(solution)/shard_map/reduce_scatter | solution.py:78
  95.6 47.0 %all-reduce.6.cloned.1.call-done = (f32[512,128]{1,0:T(8,128)}, f32[512,128]{1,0:T(8,128)}) async-done(((f32[512,128]{1,0:T(8,128)}, f32[512,128]{1,0:T(8,128)}), (f32[512,128]{1,0:T(8,128)}, f32[512,128]{1,0:T(8,128)})) %all-reduce.6.cloned.1.call-update) | async-done | bytes 524304 | tf_op jit(solution)/shard_map/psum | solution.py:86
  142.7 1.1 copy.22
  143.7 0.4 convolution_bitcast_fusion.4
  144.1 1.1 copy.20
  145.2 0.4 convolution_bitcast_fusion.5
  145.6 0.7 pad_maximum_fusion.1
  146.3 0.2 all-gather.3.cloned.1.call-start
  146.6 1.0 constant_dynamic-slice_fusion.1
  147.6 1.3 compare_convert_fusion.2
  148.9 1.2 compare_convert_fusion
  150.1 51.2 %all-reduce.4.cloned.1.call-done = f32[2,2,64,64]{2,3,1,0:T(8,128)} async-done(((f32[2,2,64,64]{2,3,1,0:T(8,128)}), f32[2,2,64,64]{2,3,1,0:T(8,128)}) %all-reduce.4.cloned.1.call-update) | async-done | bytes 65552 | tf_op jit(solution)/shard_map/psum | solution.py:89
  201.4 0.8 fusion.60
  202.3 5.8 %cholesky.107 = f32[64,64]{1,0:T(8,128)S(1)} custom-call(f32[64,64]{1,0:T(8,128)S(1)} %fusion.62), custom_call_target="Cholesky" | custom-call | tf_op jit(solution)/shard_map/jit(cholesky)/cholesky | solution.py:58
  208.2 0.6 compare_reduce_fusion
  208.8 0.7 fusion.56
  209.5 4.9 %custom-call.11 = f32[1,64,64]{1,2,0:T(8,128)S(1)} custom-call(f32[1,64,64]{2,1,0:T(8,128)S(1)} %fusion.56), custom_call_target="InvertDiagBlocksLowerTriangular" | custom-call | tf_op jit(solution)/shard_map/triangular_solve/custom-call.0 | solution.py:60
  214.5 5.8 %cholesky.96 = f32[64,64]{1,0:T(8,128)S(1)} custom-call(f32[64,64]{1,0:T(8,128)S(1)} %fusion.64), custom_call_target="Cholesky" | custom-call | tf_op jit(solution)/shard_map/jit(cholesky)/cholesky | solution.py:58
  220.4 0.6 compare_reduce_fusion.1
  221.0 0.7 fusion.55
  221.7 4.9 %custom-call.10 = f32[1,64,64]{1,2,0:T(8,128)S(1)} custom-call(f32[1,64,64]{2,1,0:T(8,128)S(1)} %fusion.55), custom_call_target="InvertDiagBlocksLowerTriangular" | custom-call | tf_op jit(solution)/shard_map/triangular_solve/custom-call.0 | solution.py:60
  226.7 5.8 %cholesky.85 = f32[64,64]{1,0:T(8,128)S(1)} custom-call(f32[64,64]{1,0:T(8,128)S(1)} %fusion.66), custom_call_target="Cholesky" | custom-call | tf_op jit(solution)/shard_map/jit(cholesky)/cholesky | solution.py:58
  232.6 0.6 compare_reduce_fusion.2
  233.2 0.7 fusion.54
  233.9 4.9 %custom-call.9 = f32[1,64,64]{1,2,0:T(8,128)S(1)} custom-call(f32[1,64,64]{2,1,0:T(8,128)S(1)} %fusion.54), custom_call_target="InvertDiagBlocksLowerTriangular" | custom-call | tf_op jit(solution)/shard_map/triangular_solve/custom-call.0 | solution.py:60
  238.9 5.8 %cholesky.74 = f32[64,64]{1,0:T(8,128)S(1)} custom-call(f32[64,64]{1,0:T(8,128)S(1)} %fusion.68), custom_call_target="Cholesky" | custom-call | tf_op jit(solution)/shard_map/jit(cholesky)/cholesky | solution.py:58
  244.7 0.6 compare_reduce_fusion.3
  245.4 0.7 fusion.53
  246.1 4.9 %custom-call.8 = f32[1,64,64]{1,2,0:T(8,128)S(1)} custom-call(f32[1,64,64]{2,1,0:T(8,128)S(1)} %fusion.53), custom_call_target="InvertDiagBlocksLowerTriangular" | custom-call | tf_op jit(solution)/shard_map/triangular_solve/custom-call.0 | solution.py:60
  251.0 0.5 convolution_bitcast_fusion
  251.5 0.4 convolution_bitcast_fusion.1
  252.0 0.5 convolution_bitcast_fusion.2
  252.5 0.4 convolution_bitcast_fusion.3
  253.0 1.0 copy.28
  254.0 30.6 %all-gather.3.cloned.1.call-done = bf16[1,4096,1024]{2,1,0:T(8,128)(2,1)} async-done(((bf16[1,512,1024]{2,1,0:T(8,128)(2,1)}), bf16[1,4096,1024]{2,1,0:T(8,128)(2,1)}) %all-gather.3.cloned.1.call-update) | async-done | bytes 8388624 | tf_op jit(solution)/shard_map/all_gather | solution.py:98
  284.6 6.9 %fusion.13 = (f32[144]{0:T(256)S(1)}, f32[144,4096]{1,0:T(8,128)S(1)}) fusion(f32[144]{0:T(256)S(1)} %bitcast.141, bf16[2,144,4096]{2,1,0:T(8,128)(2,1)} %param.10, s32[]{:T(128)S(6)} %select_n.69, f32[4096]{0:T(1024)S(1)} %bitcast.140, bf16[1,4096,1024]{2,1,0:T(8,128)(2,1)} %all-gather.3.cloned.1.call-done, bf16[2,144,1024]{2,1,0:T(8,128)(2,1)S(1)} %copy-done.4), kind=kOutput, calls=%fused_computation.16 | convolution fusion | flops 1210908544 | bytes 12241472 | tf_op jit(solution)/shard_map/dot_general | solution.py:96
  291.5 1.6 fusion.16
  (44 shorter events, 1.2 us)
Async XLA Ops:
  7.2 139.4 %copy-start = (bf16[2,512,1024]{2,1,0:T(8,128)(2,1)S(1)}, bf16[2,512,1024]{2,1,0:T(8,128)(2,1)}, u32[]{:S(2)}) copy-start(bf16[2,512,1024]{2,1,0:T(8,128)(2,1)} %param.12) | copy-start | bytes 6291460
  7.2 6.7 %copy-start.6 = (s32[2]{0:T(128)S(1)}, s32[2]{0:T(128)}, u32[]{:S(2)}) copy-start(s32[2]{0:T(128)} %param.16) | copy-start | bytes 28
  7.2 9.0 %copy-start.5 = (f32[2,4096]{1,0:T(2,128)S(1)}, f32[2,4096]{1,0:T(2,128)}, u32[]{:S(2)}) copy-start(f32[2,4096]{1,0:T(2,128)} %param.13) | copy-start | bytes 98308
  7.2 51.4 %reduce-scatter.5.cloned.1.call-start = ((), (), s32[]{:S(2)}) async-start(), calls=%async_computation.3 | async-start | bytes 2359296 | tf_op jit(solution)/shard_map/reduce_scatter | solution.py:78
  19.7 75.8 %reduce-scatter.3.cloned.1.call-start = ((), (), s32[]{:S(2)}) async-start(), calls=%async_computation.2 | async-start | bytes 2359296 | tf_op jit(solution)/shard_map/reduce_scatter | solution.py:78
  23.8 118.9 %all-reduce.6.cloned.1.call-start = ((), (), s32[]{:S(2)}) async-start(), calls=%async_computation.6 | async-start | bytes 1048576 | tf_op jit(solution)/shard_map/psum | solution.py:86
  95.6 105.8 %all-reduce.4.cloned.1.call-start = ((), (), s32[]{:S(2)}) async-start(), calls=%async_computation.4 | async-start | bytes 262144 | tf_op jit(solution)/shard_map/psum | solution.py:89
  146.3 104.7 %copy-start.3 = (f32[512,128]{1,0:T(8,128)S(1)}, f32[512,128]{1,0:T(8,128)}, u32[]{:S(2)}) copy-start(f32[512,128]{1,0:T(8,128)} %get-tuple-element.10) | copy-start | bytes 786436
  146.3 138.2 %all-gather.3.cloned.1.call-start = ((), (), s32[]{:S(2)}) async-start(), calls=%async_computation.5 | async-start | bytes 9437184 | tf_op jit(solution)/shard_map/all_gather | solution.py:98
  147.6 104.4 %copy-start.2 = (f32[512,128]{1,0:T(8,128)S(1)}, f32[512,128]{1,0:T(8,128)}, u32[]{:S(2)}) copy-start(f32[512,128]{1,0:T(8,128)} %get-tuple-element.11) | copy-start | bytes 786436
  251.0 33.6 %copy-start.4 = (bf16[2,144,1024]{2,1,0:T(8,128)(2,1)S(1)}, bf16[2,144,1024]{2,1,0:T(8,128)(2,1)}, u32[]{:S(2)}) copy-start(bf16[2,144,1024]{2,1,0:T(8,128)(2,1)} %param.11) | copy-start | bytes 1769476
  284.6 6.9 %copy-start.1 = (bf16[2,144,4096]{2,1,0:T(8,128)(2,1)S(1)}, bf16[2,144,4096]{2,1,0:T(8,128)(2,1)}, u32[]{:S(2)}) copy-start(bf16[2,144,4096]{2,1,0:T(8,128)(2,1)} %param.10) | copy-start | bytes 7077892
Sparse Core Ops, SparseCore 0:
  19.9 38.7 reduce-scatter.4
  60.9 34.6 reduce-scatter.2
  98.6 44.0 all-reduce.5
  146.4 54.8 all-reduce.3
  203.4 81.1 all-gather.2
where the time goes:
time: 300 us
  waiting for transfers between devices  201 us (67%)
  other arithmetic  59.6 us (20%)
  matrix products  17.6 us (6%)
  between operations  14.2 us (5%)
  local copies, waits for them, and re-layouts  7.26 us (2%)
    reduce_scatter x2, waiting for transfers between devices, body(): lax.psum_scatter(lax.dot_general(normed, projected, (((0,), (0,)), ((), (...  71.7 us
    psum x1, waiting for transfers between devices, body(): all_grams = lax.psum(stacked, 'fsdp')  51.2 us
    psum x1, waiting for transfers between devices, body(): factor_shard = lax.psum(local_rows, 'dp')  47 us
    all_gather x1, waiting for transfers between devices, body(): lax.all_gather(top_weight, 'fsdp', axis=0, tiled=True)  30.6 us
    another operation x12, other arithmetic, orthonormal(): lower_factor = jnp.linalg.cholesky(padded)  26.1 us
    another operation x8, other arithmetic, orthonormal(): lax.linalg.triangular_solve(lower_factor, block_cols, left_side=False, lo...  22.2 us
    dot_general x2, matrix products, body(): lax.dot_general(normed, projected, (((0,), (0,)), ((), ())), preferred_el...  6.96 us
    dot_general x1, matrix products, body(): lax.dot_general(top_grads, lax.all_gather(top_weight, 'fsdp', axis=0, til...  6.9 us
  transfers between devices with their start and end apart: 5, of which 5 were waited for; matrix products, arithmetic and copies ran while one was open for 20% of the time, Pallas kernels for 0%

commit v1 on v0

--- a/solution.py
+++ b/solution.py
@@ -1,8 +1,11 @@
+import functools
 import math
 
 import jax
 import jax.numpy as jnp
 from jax import lax
+from jax.experimental import pallas as pl
+from jax.experimental.pallas import tpu as pltpu
 from jax.sharding import PartitionSpec as P
 
 D = 4096
@@ -109,6 +112,358 @@
     return (hidden_grad, jnp.stack(basis_list))
 
 
+MESH = pl.DeviceIdType.MESH
+
+
+def fused_kernel(
+    n_z, ranks_ref, order_ref, hidden_ref, cot_ref, weight_ref, gain_ref, factor_ref,
+    grad_ref, basis_ref,
+    acc, s0_send, s0_recv, s1_send, s1_recv, s2_send, s2_recv, keep2, s3_send, s3_recv,
+    f_send, f_all, g_all, z_send, z_all, l_send, l_recv, w_all, scaled, inverse,
+    send_sem, recv_sem, f_sem, w_send, w_recv, sib_sem, own_sem,
+):
+    q = lax.axis_index("dp")
+    me = lax.axis_index("fsdp")
+    z, c = me // 2, me % 2
+    y, x = q // 2, q % 2
+    n_dp = 4
+    width = hidden_ref.shape[2]
+    tokens = hidden_ref.shape[1]
+    per_z = width // n_z
+    heads = cot_ref.shape[2] // 2
+    qrows = weight_ref.shape[1]
+    half_rows = qrows // 2
+    x_nbr = y * 2 + (1 - x)
+    y_nbr = (1 - y) * 2 + x
+    diag = (1 - y) * 2 + (1 - x)
+    sibling = (q, z * 2 + (1 - c))
+
+    def same_core(dp_index, z_index):
+        return (dp_index, z_index * 2 + c)
+
+    barrier = pltpu.get_barrier_semaphore()
+    peers = [sibling]
+    for k in range(1, n_dp):
+        for core in range(2):
+            peers.append(((q + k) % n_dp, z * 2 + core))
+    for d in range(1, n_z):
+        peers.append(same_core(q, (z + d) % n_z))
+    for peer in peers:
+        pl.semaphore_signal(barrier, inc=1, device_id=peer, device_id_type=MESH)
+    pl.semaphore_wait(barrier, len(peers))
+
+    pending = []
+
+    def send(src, dst, ssem, rsem, target):
+        copy = pltpu.make_async_remote_copy(
+            src_ref=src, dst_ref=dst, send_sem=ssem, recv_sem=rsem,
+            device_id=target, device_id_type=MESH,
+        )
+        copy.start()
+        pending.append(copy)
+        return copy
+
+    def arrived(dst, rsem):
+        pltpu.make_async_remote_copy(
+            src_ref=dst, dst_ref=dst, send_sem=rsem, recv_sem=rsem,
+            device_id=sibling, device_id_type=MESH,
+        ).wait_recv()
+
+    def piece(dp_index, z_index, offset, rows):
+        start = (z_index * 2 + c) * (n_dp * qrows) + dp_index * qrows + offset
+        return w_all.at[pl.ds(pl.multiple_of(start, half_rows), rows)]
+
+    w_count = [0]
+
+    def w_copy(src, dst, rsem, target):
+        send(src, dst, w_send.at[w_count[0]], rsem, target)
+        w_count[0] += 1
+
+    for d in range(1, n_z):
+        w_copy(weight_ref.at[q], piece(q, z, 0, qrows), w_recv.at[0, d - 1], same_core(q, (z + d) % n_z))
+    own_copies = []
+    for k in range(n_dp):
+        own = pltpu.make_async_copy(weight_ref.at[k], piece(k, z, 0, qrows), own_sem.at[k])
+        own.start()
+        own_copies.append(own)
+
+    lane = lax.broadcasted_iota(jnp.int32, (1, 128), 1)
+
+    def slot_sums(slot, store):
+        limit = jnp.where(lane < 64, ranks_ref[2 * slot], ranks_ref[2 * slot + 1])
+        kept = jnp.where(lane % 64 < limit, factor_ref[slot].astype(jnp.float32), 0.0).astype(jnp.bfloat16)
+        keys_part = jnp.dot(cot_ref[slot, :, :heads], kept, preferred_element_type=jnp.float32)
+        values_part = jnp.dot(cot_ref[slot, :, heads:], kept, preferred_element_type=jnp.float32)
+        projected = jnp.where(lane < 64, keys_part, values_part).astype(jnp.bfloat16)
+        total = jnp.zeros((tokens, 1), jnp.float32)
+        for part in range(n_z):
+            wide = hidden_ref[slot, :, part * per_z : (part + 1) * per_z].astype(jnp.float32)
+            total += jnp.sum(wide * wide, axis=1, keepdims=True)
+        inv = lax.rsqrt(total / width + 1e-05)
+        inverse[slot] = inv
+        flipped = projected.astype(jnp.float32).T.astype(jnp.bfloat16)
+        for part in range(n_z):
+            cols = slice(part * per_z, (part + 1) * per_z)
+            wide = hidden_ref[slot, :, cols].astype(jnp.float32)
+            gain = gain_ref[pl.ds(slot, 1), cols]
+            normed = (wide * inv * gain).astype(jnp.bfloat16)
+            sums = jnp.dot(flipped, normed, preferred_element_type=jnp.float32)
+            for yy in range(2):
+                for xx in range(2):
+                    for h in range(2):
+                        first, second = (xx, yy) if h == 0 else (yy, xx)
+                        at = (yy * 2 + xx) * 256 + h * 128
+                        store(h, first, second, part, sums[:, at : at + 128])
+
+    def store_other(h, first, second, part, block):
+        s0_send[h, first, second, part] = block.astype(jnp.bfloat16)
+
+    def store_mine(h, first, second, part, block):
+        acc[h, first, second, part] = block
+
+    slot_sums(1 - c, store_other)
+    for h in range(2):
+        send(s0_send.at[h], s0_recv.at[h], send_sem.at[h], recv_sem.at[h], sibling)
+    slot_sums(c, store_mine)
+
+    firsts, seconds = (x, y), (y, x)
+    first_nbr, second_nbr = (x_nbr, y_nbr), (y_nbr, x_nbr)
+    for h in range(2):
+        a = firsts[h]
+        arrived(s0_recv.at[h], recv_sem.at[h])
+        s1_send[h] = (acc[h, 1 - a] + s0_recv[h, 1 - a].astype(jnp.float32)).astype(jnp.bfloat16)
+        send(s1_send.at[h], s1_recv.at[h], send_sem.at[2 + h], recv_sem.at[2 + h], same_core(first_nbr[h], z))
+    for h in range(2):
+        a = firsts[h]
+        acc[h, a] = acc[h, a] + s0_recv[h, a].astype(jnp.float32)
+    for h in range(2):
+        a, b = firsts[h], seconds[h]
+        arrived(s1_recv.at[h], recv_sem.at[2 + h])
+        s2_send[h] = (acc[h, a, 1 - b] + s1_recv[h, 1 - b].astype(jnp.float32)).astype(jnp.bfloat16)
+        send(s2_send.at[h], s2_recv.at[h], send_sem.at[4 + h], recv_sem.at[4 + h], same_core(second_nbr[h], z))
+    for h in range(2):
+        a, b = firsts[h], seconds[h]
+        keep2[h] = acc[h, a, b] + s1_recv[h, b].astype(jnp.float32)
+    for h in range(2):
+        arrived(s2_recv.at[h], recv_sem.at[4 + h])
+        summed = keep2[h] + s2_recv[h].astype(jnp.float32)
+        keep2[h] = summed
+        for part in range(n_z):
+            s3_send[part, h] = summed[part].astype(jnp.bfloat16)
+    for d in range(1, n_z):
+        to = (z + d) % n_z
+        send(s3_send.at[to], s3_recv.at[z], send_sem.at[5 + d], recv_sem.at[5 + d], same_core(q, to))
+    finals = [keep2[h, z] for h in range(2)]
+    for d in range(1, n_z):
+        source = (z + n_z - d) % n_z
+        arrived(s3_recv.at[source], recv_sem.at[5 + d])
+        for h in range(2):
+            finals[h] = finals[h] + s3_recv[source, h].astype(jnp.float32)
+
+    gram = jnp.zeros((128, 128), jnp.float32)
+    for h in range(2):
+        gram += lax.dot_general(
+            finals[h], finals[h], (((1,), (1,)), ((), ())),
+            precision=lax.Precision.HIGHEST, preferred_element_type=jnp.float32,
+        )
+    g_all[q] = jnp.where(lane < 64, gram[0:64, :], gram[64:128, :])
+    for k in range(1, n_dp):
+        send(g_all.at[q], g_all.at[q], send_sem.at[8 + k], recv_sem.at[8 + k], same_core((q + k) % n_dp, z))
+
+    for h in range(2):
+        f_send[h] = finals[h].astype(jnp.bfloat16)
+    f_dst = f_all.at[c, x]
+    for k in range(1, n_dp):
+        send(f_send, f_dst, send_sem.at[12 + k], f_sem.at[c, x], ((q + k) % n_dp, z * 2 + y))
+    local = pltpu.make_async_copy(f_send, f_dst, f_sem.at[c, x])
+    to_sibling = pltpu.make_async_remote_copy(
+        src_ref=f_send, dst_ref=f_dst, send_sem=send_sem.at[16], recv_sem=f_sem.at[c, x],
+        device_id=sibling, device_id_type=MESH,
+    )
+
+    @pl.when(y == c)
+    def _():
+        local.start()
+
+    @pl.when(y != c)
+    def _():
+        to_sibling.start()
+
+    for own in own_copies:
+        own.wait()
+    for k in range(n_dp):
+        w_copy(weight_ref.at[k], piece(k, z, 0, qrows), sib_sem, sibling)
+    for d in range(1, n_z):
+        source = (z + n_z - d) % n_z
+        block = piece(q, source, 0, qrows)
+        arrived(block, w_recv.at[0, d - 1])
+        w_copy(block, block, w_recv.at[1, d - 1], same_core(x_nbr, z))
+        w_copy(block, block, w_recv.at[2, d - 1], same_core(y_nbr, z))
+        w_copy(block, block, sib_sem, sibling)
+
+    def relay(d):
+        source = (z + n_z - d) % n_z
+        for kind, origin, onward, offset in ((1, x_nbr, y_nbr, 0), (2, y_nbr, x_nbr, half_rows)):
+            block = piece(origin, source, 0, qrows)
+            arrived(block, w_recv.at[kind, d - 1])
+            part = piece(origin, source, offset, half_rows)
+            w_copy(part, part, w_recv.at[2 + kind, d - 1], same_core(onward, z))
+            w_copy(block, block, sib_sem, sibling)
+
+    for k in range(1, n_dp):
+        source = (q + n_dp - k) % n_dp
+        arrived(g_all.at[source], recv_sem.at[8 + k])
+    plane = g_all[0] + g_all[1] + g_all[2] + g_all[3]
+    z_all[z] = plane
+    for d in range(1, n_z):
+        send(z_all.at[z], z_all.at[z], send_sem.at[16 + d], recv_sem.at[16 + d], same_core(q, (z + d) % n_z))
+    for d in range(1, n_z):
+        arrived(z_all.at[(z + n_z - d) % n_z], recv_sem.at[16 + d])
+    matrix = z_all[0]
+    for part in range(1, n_z):
+        matrix += z_all[part]
+
+    row = lax.broadcasted_iota(jnp.int32, (64, 128), 0)
+    column = lax.broadcasted_iota(jnp.int32, (64, 128), 1)
+    left = column < 64
+    limit = jnp.where(left, ranks_ref[2 * c], ranks_ref[2 * c + 1])
+    on_diagonal = row == column % 64
+    matrix = matrix + jnp.where(on_diagonal & (row >= limit), 1.0, 0.0)
+    unit = jnp.where(on_diagonal, 1.0, 0.0)
+    for j in range(64):
+        pivot_row = matrix[j : j + 1, :]
+        pivot = jnp.where(lane < 64, matrix[j : j + 1, j : j + 1], matrix[j : j + 1, 64 + j : 65 + j])
+        scale = 1.0 / pivot
+        factor = jnp.where(left, matrix[:, j : j + 1], matrix[:, 64 + j : 65 + j])
+        factor = jnp.where(row > j, factor, 0.0)
+        unit_row = unit[j : j + 1, :]
+        matrix = matrix - factor * (pivot_row * scale)
+        unit = unit - factor * (unit_row * scale)
+        if j in (20, 40):
+            relay(j // 20)
+    relay(3) if n_z > 3 else None
+    pivots = jnp.where(on_diagonal, matrix, 0.0)
+    left_pivot = jnp.sum(jnp.where(left, pivots, 0.0), axis=1, keepdims=True)
+    right_pivot = jnp.sum(jnp.where(left, 0.0, pivots), axis=1, keepdims=True)
+    l_send[...] = unit * (math.sqrt(width) * jnp.where(left, lax.rsqrt(left_pivot), lax.rsqrt(right_pivot)))
+    send(l_send, l_recv, send_sem.at[20], recv_sem.at[20], sibling)
+    arrived(l_recv, recv_sem.at[20])
+
+    for i in range(2):
+        for s in range(2):
+            arrived(f_all.at[s, i], f_sem.at[s, i])
+    for s in range(2):
+        packed = jnp.where(s == c, l_send[...], l_recv[...])
+        block = jnp.concatenate([jnp.where(left, packed, 0.0), jnp.where(left, 0.0, packed)], axis=0)
+        high = block.astype(jnp.bfloat16)
+        low = (block - high.astype(jnp.float32)).astype(jnp.bfloat16)
+        for i in range(2):
+            for h in range(2):
+                rows = f_all[s, i, h]
+                turned = jnp.dot(high, rows, preferred_element_type=jnp.float32)
+                turned += jnp.dot(low, rows, preferred_element_type=jnp.float32)
+                at = i * 256 + h * 128
+                basis_ref[s, at : at + 128, :] = turned.T
+
+    for d in range(1, n_z):
+        source = (z + n_z - d) % n_z
+        for kind, offset in ((3, 0), (4, half_rows)):
+            part = piece(diag, source, offset, half_rows)
+            arrived(part, w_recv.at[kind, d - 1])
+            w_copy(part, part, sib_sem, sibling)
+    arrived(w_all.at[0 : w_all.shape[0] // 2], sib_sem)
+
+    top = order_ref[0]
+    tile = 512
+    top_inverse = inverse[top]
+
+    def columns(step, inner):
+        at = pl.multiple_of(step * tile, tile)
+        product = lax.dot_general(
+            cot_ref[top], w_all[pl.ds(at, tile), :], (((1,), (1,)), ((), ())),
+            preferred_element_type=jnp.float32,
+        )
+        product = product * gain_ref[pl.ds(top, 1), pl.ds(at, tile)]
+        scaled[:, pl.ds(at, tile)] = product
+        unit_rows = hidden_ref[top, :, pl.ds(at, tile)].astype(jnp.float32) * top_inverse
+        return inner + jnp.sum(product * unit_rows, axis=1, keepdims=True)
+
+    inner = lax.fori_loop(0, width // tile, columns, jnp.zeros((tokens, 1), jnp.float32))
+    inner_mean = inner / width
+
+    def finish(step, carry):
+        at = pl.multiple_of(step * tile, tile)
+        unit_rows = hidden_ref[top, :, pl.ds(at, tile)].astype(jnp.float32) * top_inverse
+        grad_ref[:, pl.ds(at, tile)] = (
+            top_inverse * (scaled[:, pl.ds(at, tile)] - unit_rows * inner_mean)
+        ).astype(jnp.bfloat16)
+        return carry
+
+    lax.fori_loop(0, width // tile, finish, 0)
+
+    for copy in pending:
+        copy.wait_send()
+
+    @pl.when(y != c)
+    def _():
+        to_sibling.wait_send()
+
+
+def fused_body(n_dp, n_fsdp, hidden, cotangent, proj_weight, norm_gain, prev_factor, factor_ranks, layer_order):
+    layers, tokens, width = hidden.shape
+    n_z = n_fsdp // 2
+    kv = cotangent.shape[2]
+    owned = width // n_fsdp
+    top_weight = lax.dynamic_index_in_dim(proj_weight, layer_order[0], 0, keepdims=False)
+    top_weight = top_weight.reshape(n_dp, owned // n_dp, kv)
+    vmem = pl.BlockSpec(memory_space=pltpu.VMEM)
+    smem = pl.BlockSpec(memory_space=pltpu.SMEM)
+    half = jnp.bfloat16
+    full = jnp.float32
+    dma = pltpu.SemaphoreType.DMA
+    return pl.pallas_call(
+        functools.partial(fused_kernel, n_z),
+        out_shape=(
+            jax.ShapeDtypeStruct((tokens, width), half),
+            jax.ShapeDtypeStruct((layers, owned, prev_factor.shape[2]), full),
+        ),
+        in_specs=[smem, smem] + [vmem] * 5,
+        out_specs=(vmem, vmem),
+        scratch_shapes=[
+            pltpu.VMEM((2, 2, 2, n_z, 128, 128), full),
+            pltpu.VMEM((2, 2, 2, n_z, 128, 128), half),
+            pltpu.VMEM((2, 2, 2, n_z, 128, 128), half),
+            pltpu.VMEM((2, 2, n_z, 128, 128), half),
+            pltpu.VMEM((2, 2, n_z, 128, 128), half),
+            pltpu.VMEM((2, n_z, 128, 128), half),
+            pltpu.VMEM((2, n_z, 128, 128), half),
+            pltpu.VMEM((2, n_z, 128, 128), full),
+            pltpu.VMEM((n_z, 2, 128, 128), half),
+            pltpu.VMEM((n_z, 2, 128, 128), half),
+            pltpu.VMEM((2, 128, 128), half),
+            pltpu.VMEM((2, 2, 2, 128, 128), half),
+            pltpu.VMEM((4, 64, 128), full),
+            pltpu.VMEM((8, 128), full),
+            pltpu.VMEM((n_z, 64, 128), full),
+            pltpu.VMEM((64, 128), full),
+            pltpu.VMEM((64, 128), full),
+            pltpu.VMEM((width, kv), half),
+            pltpu.VMEM((tokens, width), full),
+            pltpu.VMEM((2, tokens, 1), full),
+            dma((24,)),
+            dma((24,)),
+            dma((2, 2)),
+            dma((64,)),
+            dma((5, n_z)),
+            dma,
+            dma((4,)),
+        ],
+        compiler_params=pltpu.CompilerParams(
+            collective_id=0, has_side_effects=True, vmem_limit_bytes=60 * 1024 * 1024
+        ),
+    )(factor_ranks.reshape(-1), layer_order, hidden, cotangent, top_weight, norm_gain, prev_factor)
+
+
 def solution(mesh):
     in_specs = (
         P(None, ("dp", "fsdp"), None),
@@ -120,4 +475,8 @@
         P(),
     )
     out_specs = (P(("dp", "fsdp"), None), P(None, "fsdp", None))
-    return jax.shard_map(body, mesh=mesh, in_specs=in_specs, out_specs=out_specs, check_vma=False)
+    n_dp, n_fsdp = mesh.shape["dp"], mesh.shape["fsdp"]
+    step = body
+    if n_dp == 4 and n_fsdp % 2 == 0 and D // (n_dp * n_fsdp // 2) == 2 * 128:
+        step = functools.partial(fused_body, n_dp, n_fsdp)
+    return jax.shard_map(step, mesh=mesh, in_specs=in_specs, out_specs=out_specs, check_vma=False)

time: 300 us -> 85.1 us (0.28)
  waiting for transfers between devices: 201 us -> 0 us
  Pallas kernels: 0 us -> 75.7 us
  other arithmetic: 59.6 us -> 0 us
  matrix products: 17.6 us -> 0 us
  between operations: 14.2 us -> 2.74 us
    psum x2 -> x0, waiting for transfers between devices: 98.2 us -> none  [the longest x1 51.2 us: body(): all_grams = lax.psum(stacked, 'fsdp')]
    pallas_call x0 -> x1, Pallas kernels: none -> 75.7 us  [fused_body(): pl.pallas_call(functools.partial(fused_kernel, n_z), out_shape=(jax.Shape...]
    reduce_scatter x2 -> x0, waiting for transfers between devices: 71.7 us -> none  [body(): lax.psum_scatter(lax.dot_general(normed, projected, (((0,), (0,)), ((), (...]
    another operation x23 -> x0, other arithmetic: 49 us -> none  [the longest x12 26.1 us: orthonormal(): lower_factor = jnp.linalg.cholesky(padded)]
    all_gather x1 -> x0, waiting for transfers between devices: 30.6 us -> none  [body(): lax.all_gather(top_weight, 'fsdp', axis=0, tiled=True)]
    dot_general x9 -> x0, matrix products: 15.7 us -> none  [the longest x2 6.96 us: body(): lax.dot_general(normed, projected, (((0,), (0,)), ((), ())), preferred_el...]
    convert_element_type x3 -> x0, other arithmetic: 4.04 us -> none  [the longest x2 2.46 us: orthonormal(): (column >= rank_pair[member]).astype(jnp.float32)]
  transfers between devices with their start and end apart: 5 -> 0, of which waited for: 5 -> 0; matrix products, arithmetic and copies ran while one was open for 20% -> 0% of each run, Pallas kernels for 0% -> 0%
where the time goes in v1:
time: 85.1 us; the launch traced here: 84 us
  Pallas kernels  75.7 us (89%)
  local copies, waits for them, and re-layouts  5.56 us (7%)
  between operations  2.74 us (3%)
    pallas_call x1, Pallas kernels, fused_body(): pl.pallas_call(functools.partial(fused_kernel, n_z), out_shape=(jax.Shape...  75.7 us
    unnamed x6, local copies, waits for them, and re-layouts  3.25 us

profile of v1, /device:TPU:0, one launch (start us, length us, event | category | flops | bytes accessed | tf_op | source)
XLA Modules:
  0.0 84.0 jit_solution(5450753340645968819)
XLA Ops:
  0.6 0.0 copy-start
  2.7 1.3 %reshape.11.ranks_ref = s32[4]{0:T(128)} reshape(s32[2,2]{1,0:T(2,128)} %param.12) | data formatting | bytes 32 | tf_op jit(solution)/shard_map/reshape | solution.py:464
  4.0 0.0 copy-done
  4.0 1.0 %constant_dynamic-slice_fusion = bf16[1,512,1024]{2,1,0:T(8,128)(2,1)} fusion(bf16[2,512,1024]{2,1,0:T(8,128)(2,1)S(1)} %copy-done, s32[]{:T(128)S(6)} %select_n.4), kind=kLoop, calls=%fused_computation | loop fusion | bytes 2097156 | tf_op jit(solution)/shard_map/jit(dynamic_index_in_dim)/dynamic_slice | solution.py:417
  5.0 75.7 %shard_map.86 = (bf16[144,4096]{1,0:T(8,128)(2,1)}, f32[2,512,128]{2,1,0:T(8,128)}) custom-call(s32[4]{0:T(128)} %reshape.11.ranks_ref, s32[2]{0:T(128)} %order_ref.1, bf16[2,144,4096]{2,1,0:T(8,128)(2,1)} %hidden_ref.1, bf16[2,144,1024]{2,1,0:T(8,128)(2,1)} %cot_ref.1, bf16[4,128,1024]{2,1,0:T(8,128)(2,1)} %bitcast.3, f32[2,4096]{1,0:T(2,128)} %gain_ref.1, ...), custom_call_target="tpu_custom_call" | custom-call | tf_op jit(solution)/shard_map/pallas_call | solution.py:424
  80.8 0.0 copy-start.1
  80.8 2.4 %copy.11 = bf16[144,4096]{1,0:T(8,128)(2,1)} copy(bf16[144,4096]{1,0:T(8,128)(2,1)} %get-tuple-element.4) | data formatting | bytes 2359296
  83.2 0.0 copy-done.1
  83.2 0.8 copy.12
Async XLA Ops:
  0.6 3.4 %copy-start = (bf16[2,512,1024]{2,1,0:T(8,128)(2,1)S(1)}, bf16[2,512,1024]{2,1,0:T(8,128)(2,1)}, u32[]{:S(2)}) copy-start(bf16[2,512,1024]{2,1,0:T(8,128)(2,1)} %param.9) | copy-start | bytes 6291460
  80.8 2.5 %copy-start.1 = (f32[2,512,128]{2,1,0:T(8,128)S(1)}, f32[2,512,128]{2,1,0:T(8,128)}, u32[]{:S(2)}) copy-start(f32[2,512,128]{2,1,0:T(8,128)} %get-tuple-element.5) | copy-start | bytes 1572868

commit v2 on v1

--- a/solution.py
+++ b/solution.py
@@ -117,9 +117,9 @@
 
 def fused_kernel(
     n_z, ranks_ref, order_ref, hidden_ref, cot_ref, weight_ref, gain_ref, factor_ref,
-    grad_ref, basis_ref,
+    scaled_ref, rows_ref, basis_ref,
     acc, s0_send, s0_recv, s1_send, s1_recv, s2_send, s2_recv, keep2, s3_send, s3_recv,
-    f_send, f_all, g_all, z_send, z_all, l_send, l_recv, w_all, scaled, inverse,
+    f_send, f_all, g_all, z_send, z_all, l_send, l_recv, w_all, inverse,
     send_sem, recv_sem, f_sem, w_send, w_recv, sib_sem, own_sem,
 ):
     q = lax.axis_index("dp")
@@ -131,7 +131,8 @@
     tokens = hidden_ref.shape[1]
     per_z = width // n_z
     heads = cot_ref.shape[2] // 2
-    qrows = weight_ref.shape[1]
+    own_rows = weight_ref.shape[0]
+    qrows = own_rows // 4
     half_rows = qrows // 2
     x_nbr = y * 2 + (1 - x)
     y_nbr = (1 - y) * 2 + x
@@ -173,24 +174,89 @@
         start = (z_index * 2 + c) * (n_dp * qrows) + dp_index * qrows + offset
         return w_all.at[pl.ds(pl.multiple_of(start, half_rows), rows)]
 
+    far = (2 * z) // n_z
+    near = z + far * (n_z - 1 - 2 * z)
+
+    def physical(index):
+        return index + far * (n_z - 1 - 2 * index)
+
+    def source_of(k):
+        return physical(k + (k + n_z - near) // n_z)
+
+    inside = near != 0
+    guarded = []
     w_count = [0]
 
-    def w_copy(src, dst, rsem, target):
-        send(src, dst, w_send.at[w_count[0]], rsem, target)
+    def w_copy(src, dst, rsem, target, when=None):
+        ssem = w_send.at[w_count[0]]
         w_count[0] += 1
-
-    for d in range(1, n_z):
-        w_copy(weight_ref.at[q], piece(q, z, 0, qrows), w_recv.at[0, d - 1], same_core(q, (z + d) % n_z))
-    own_copies = []
-    for k in range(n_dp):
-        own = pltpu.make_async_copy(weight_ref.at[k], piece(k, z, 0, qrows), own_sem.at[k])
-        own.start()
-        own_copies.append(own)
+        if when is None:
+            send(src, dst, ssem, rsem, target)
+            return
+        copy = pltpu.make_async_remote_copy(
+            src_ref=src, dst_ref=dst, send_sem=ssem, recv_sem=rsem,
+            device_id=target, device_id_type=MESH,
+        )
+
+        @pl.when(when)
+        def _():
+            copy.start()
+
+        guarded.append((when, copy))
+
+    own_quarter = weight_ref.at[pl.ds(pl.multiple_of(q * qrows, qrows), qrows)]
+    w_copy(own_quarter, piece(q, z, 0, qrows), w_recv.at[0, z], same_core(q, physical(near + 1)))
+    w_copy(own_quarter, piece(q, z, 0, qrows), w_recv.at[0, z], same_core(q, physical((near + n_z - 1) % n_z)), inside)
+
+    def along_z(k):
+        source = source_of(k)
+        block = piece(q, source, 0, qrows)
+        arrived(block, w_recv.at[0, source])
+        onward = near + 1 if k == 0 else (near + n_z - 1) % n_z
+        w_copy(block, block, w_recv.at[0, source], same_core(q, physical(onward)), inside)
+
+    def in_plane(k):
+        block = piece(q, source_of(k), 0, qrows)
+        w_copy(block, block, w_recv.at[1, k], same_core(x_nbr, z))
+        w_copy(block, block, w_recv.at[2, k], same_core(y_nbr, z))
+        w_copy(block, block, sib_sem.at[1 + k], sibling)
+
+    def relay(k):
+        source = source_of(k)
+        for kind, origin, onward, offset in ((1, x_nbr, y_nbr, 0), (2, y_nbr, x_nbr, half_rows)):
+            block = piece(origin, source, 0, qrows)
+            arrived(block, w_recv.at[kind, k])
+            part = piece(origin, source, offset, half_rows)
+            w_copy(part, part, w_recv.at[2 + kind, k], same_core(onward, z))
+            w_copy(block, block, sib_sem.at[1 + k], sibling)
+
+    def last_leg(k):
+        source = source_of(k)
+        for kind, offset in ((3, 0), (4, half_rows)):
+            part = piece(diag, source, offset, half_rows)
+            arrived(part, w_recv.at[kind, k])
+            w_copy(part, part, sib_sem.at[1 + k], sibling)
+
+    top = order_ref[0]
+
+    def gradient_columns(source, slot_sem, inner):
+        arrived(w_all.at[0:own_rows], slot_sem)
+        for core in range(2):
+            at = pl.multiple_of((source * 2 + core) * own_rows, own_rows)
+            product = lax.dot_general(
+                cot_ref[top], w_all[pl.ds(at, own_rows), :], (((1,), (1,)), ((), ())),
+                preferred_element_type=jnp.float32,
+            )
+            product = product * gain_ref[pl.ds(top, 1), pl.ds(at, own_rows)]
+            scaled_ref[:, pl.ds(at, own_rows)] = product
+            unit_rows = hidden_ref[top, :, pl.ds(at, own_rows)].astype(jnp.float32) * inverse[top]
+            inner = inner + jnp.sum(product * unit_rows, axis=1, keepdims=True)
+        return inner
 
     lane = lax.broadcasted_iota(jnp.int32, (1, 128), 1)
 
     def slot_sums(slot, store):
-        limit = jnp.where(lane < 64, ranks_ref[2 * slot], ranks_ref[2 * slot + 1])
+        limit = jnp.where(lane < 64, ranks_ref[slot, 0], ranks_ref[slot, 1])
         kept = jnp.where(lane % 64 < limit, factor_ref[slot].astype(jnp.float32), 0.0).astype(jnp.bfloat16)
         keys_part = jnp.dot(cot_ref[slot, :, :heads], kept, preferred_element_type=jnp.float32)
         values_part = jnp.dot(cot_ref[slot, :, heads:], kept, preferred_element_type=jnp.float32)
@@ -225,6 +291,10 @@
     for h in range(2):
         send(s0_send.at[h], s0_recv.at[h], send_sem.at[h], recv_sem.at[h], sibling)
     slot_sums(c, store_mine)
+    own_place = piece(0, z, 0, own_rows)
+    own_copy = pltpu.make_async_copy(weight_ref, own_place, own_sem)
+    own_copy.start()
+    w_copy(weight_ref, own_place, sib_sem.at[0], sibling)
 
     firsts, seconds = (x, y), (y, x)
     first_nbr, second_nbr = (x_nbr, y_nbr), (y_nbr, x_nbr)
@@ -236,6 +306,7 @@
     for h in range(2):
         a = firsts[h]
         acc[h, a] = acc[h, a] + s0_recv[h, a].astype(jnp.float32)
+    along_z(0)
     for h in range(2):
         a, b = firsts[h], seconds[h]
         arrived(s1_recv.at[h], recv_sem.at[2 + h])
@@ -244,6 +315,8 @@
     for h in range(2):
         a, b = firsts[h], seconds[h]
         keep2[h] = acc[h, a, b] + s1_recv[h, b].astype(jnp.float32)
+    in_plane(0)
+    along_z(1)
     for h in range(2):
         arrived(s2_recv.at[h], recv_sem.at[4 + h])
         summed = keep2[h] + s2_recv[h].astype(jnp.float32)
@@ -253,6 +326,7 @@
     for d in range(1, n_z):
         to = (z + d) % n_z
         send(s3_send.at[to], s3_recv.at[z], send_sem.at[5 + d], recv_sem.at[5 + d], same_core(q, to))
+    along_z(2)
     finals = [keep2[h, z] for h in range(2)]
     for d in range(1, n_z):
         source = (z + n_z - d) % n_z
@@ -289,26 +363,10 @@
     def _():
         to_sibling.start()
 
-    for own in own_copies:
-        own.wait()
-    for k in range(n_dp):
-        w_copy(weight_ref.at[k], piece(k, z, 0, qrows), sib_sem, sibling)
-    for d in range(1, n_z):
-        source = (z + n_z - d) % n_z
-        block = piece(q, source, 0, qrows)
-        arrived(block, w_recv.at[0, d - 1])
-        w_copy(block, block, w_recv.at[1, d - 1], same_core(x_nbr, z))
-        w_copy(block, block, w_recv.at[2, d - 1], same_core(y_nbr, z))
-        w_copy(block, block, sib_sem, sibling)
-
-    def relay(d):
-        source = (z + n_z - d) % n_z
-        for kind, origin, onward, offset in ((1, x_nbr, y_nbr, 0), (2, y_nbr, x_nbr, half_rows)):
-            block = piece(origin, source, 0, qrows)
-            arrived(block, w_recv.at[kind, d - 1])
-            part = piece(origin, source, offset, half_rows)
-            w_copy(part, part, w_recv.at[2 + kind, d - 1], same_core(onward, z))
-            w_copy(block, block, sib_sem, sibling)
+    in_plane(1)
+    in_plane(2)
+    own_copy.wait()
+    inner = gradient_columns(z, sib_sem.at[0], jnp.zeros((tokens, 1), jnp.float32))
 
     for k in range(1, n_dp):
         source = (q + n_dp - k) % n_dp
@@ -326,7 +384,7 @@
     row = lax.broadcasted_iota(jnp.int32, (64, 128), 0)
     column = lax.broadcasted_iota(jnp.int32, (64, 128), 1)
     left = column < 64
-    limit = jnp.where(left, ranks_ref[2 * c], ranks_ref[2 * c + 1])
+    limit = jnp.where(left, ranks_ref[c, 0], ranks_ref[c, 1])
     on_diagonal = row == column % 64
     matrix = matrix + jnp.where(on_diagonal & (row >= limit), 1.0, 0.0)
     unit = jnp.where(on_diagonal, 1.0, 0.0)
@@ -339,9 +397,11 @@
         unit_row = unit[j : j + 1, :]
         matrix = matrix - factor * (pivot_row * scale)
         unit = unit - factor * (unit_row * scale)
-        if j in (20, 40):
-            relay(j // 20)
-    relay(3) if n_z > 3 else None
+        if j == 20:
+            relay(0)
+        if j == 40:
+            relay(1)
+    last_leg(0)
     pivots = jnp.where(on_diagonal, matrix, 0.0)
     left_pivot = jnp.sum(jnp.where(left, pivots, 0.0), axis=1, keepdims=True)
     right_pivot = jnp.sum(jnp.where(left, 0.0, pivots), axis=1, keepdims=True)
@@ -365,44 +425,20 @@
                 at = i * 256 + h * 128
                 basis_ref[s, at : at + 128, :] = turned.T
 
-    for d in range(1, n_z):
-        source = (z + n_z - d) % n_z
-        for kind, offset in ((3, 0), (4, half_rows)):
-            part = piece(diag, source, offset, half_rows)
-            arrived(part, w_recv.at[kind, d - 1])
-            w_copy(part, part, sib_sem, sibling)
-    arrived(w_all.at[0 : w_all.shape[0] // 2], sib_sem)
-
-    top = order_ref[0]
-    tile = 512
-    top_inverse = inverse[top]
-
-    def columns(step, inner):
-        at = pl.multiple_of(step * tile, tile)
-        product = lax.dot_general(
-            cot_ref[top], w_all[pl.ds(at, tile), :], (((1,), (1,)), ((), ())),
-            preferred_element_type=jnp.float32,
-        )
-        product = product * gain_ref[pl.ds(top, 1), pl.ds(at, tile)]
-        scaled[:, pl.ds(at, tile)] = product
-        unit_rows = hidden_ref[top, :, pl.ds(at, tile)].astype(jnp.float32) * top_inverse
-        return inner + jnp.sum(product * unit_rows, axis=1, keepdims=True)
-
-    inner = lax.fori_loop(0, width // tile, columns, jnp.zeros((tokens, 1), jnp.float32))
-    inner_mean = inner / width
-
-    def finish(step, carry):
-        at = pl.multiple_of(step * tile, tile)
-        unit_rows = hidden_ref[top, :, pl.ds(at, tile)].astype(jnp.float32) * top_inverse
-        grad_ref[:, pl.ds(at, tile)] = (
-            top_inverse * (scaled[:, pl.ds(at, tile)] - unit_rows * inner_mean)
-        ).astype(jnp.bfloat16)
-        return carry
-
-    lax.fori_loop(0, width // tile, finish, 0)
+    inner = gradient_columns(source_of(0), sib_sem.at[1], inner)
+    relay(2)
+    last_leg(1)
+    inner = gradient_columns(source_of(1), sib_sem.at[2], inner)
+    last_leg(2)
+    inner = gradient_columns(source_of(2), sib_sem.at[3], inner)
+    rows_ref[0] = jnp.broadcast_to(inner / width, (tokens, 128))
+    rows_ref[1] = jnp.broadcast_to(inverse[top], (tokens, 128))
 
     for copy in pending:
         copy.wait_send()
+
+    for when, copy in guarded:
+        pl.when(when)(copy.wait_send)
 
     @pl.when(y != c)
     def _():
@@ -415,20 +451,20 @@
     kv = cotangent.shape[2]
     owned = width // n_fsdp
     top_weight = lax.dynamic_index_in_dim(proj_weight, layer_order[0], 0, keepdims=False)
-    top_weight = top_weight.reshape(n_dp, owned // n_dp, kv)
     vmem = pl.BlockSpec(memory_space=pltpu.VMEM)
     smem = pl.BlockSpec(memory_space=pltpu.SMEM)
     half = jnp.bfloat16
     full = jnp.float32
     dma = pltpu.SemaphoreType.DMA
-    return pl.pallas_call(
+    scaled, rows, basis = pl.pallas_call(
         functools.partial(fused_kernel, n_z),
         out_shape=(
-            jax.ShapeDtypeStruct((tokens, width), half),
+            jax.ShapeDtypeStruct((tokens, width), full),
+            jax.ShapeDtypeStruct((2, tokens, 128), full),
             jax.ShapeDtypeStruct((layers, owned, prev_factor.shape[2]), full),
         ),
         in_specs=[smem, smem] + [vmem] * 5,
-        out_specs=(vmem, vmem),
+        out_specs=(vmem, vmem, vmem),
         scratch_shapes=[
             pltpu.VMEM((2, 2, 2, n_z, 128, 128), full),
             pltpu.VMEM((2, 2, 2, n_z, 128, 128), half),
@@ -448,20 +484,23 @@
             pltpu.VMEM((64, 128), full),
             pltpu.VMEM((64, 128), full),
             pltpu.VMEM((width, kv), half),
-            pltpu.VMEM((tokens, width), full),
             pltpu.VMEM((2, tokens, 1), full),
             dma((24,)),
             dma((24,)),
             dma((2, 2)),
             dma((64,)),
             dma((5, n_z)),
+            dma((4,)),
             dma,
-            dma((4,)),
         ],
         compiler_params=pltpu.CompilerParams(
             collective_id=0, has_side_effects=True, vmem_limit_bytes=60 * 1024 * 1024
         ),
-    )(factor_ranks.reshape(-1), layer_order, hidden, cotangent, top_weight, norm_gain, prev_factor)
+    )(factor_ranks, layer_order, hidden, cotangent, top_weight, norm_gain, prev_factor)
+    top_hidden = lax.dynamic_index_in_dim(hidden, layer_order[0], 0, keepdims=False).astype(full)
+    inner_mean, top_inverse = rows[0, :, :1], rows[1, :, :1]
+    hidden_grad = top_inverse * (scaled - top_hidden * top_inverse * inner_mean)
+    return (hidden_grad.astype(half), basis)
 
 
 def solution(mesh):

time: 85.1 us -> 78.5 us (0.922)
  Pallas kernels: 75.7 us -> 69 us
  other arithmetic: 0 us -> 3.61 us
  local copies, waits for them, and re-layouts: 5.56 us -> 2.91 us
    pallas_call x1, Pallas kernels: 75.7 us -> 69 us  [fused_body(): pl.pallas_call(functools.partial(fused_kernel, n_z), out_shape=(jax.Shape...]
    convert_element_type x0 -> x1, other arithmetic: none -> 3.61 us  [fused_body(): return (hidden_grad.astype(half), basis)]
    unnamed x6 -> x5, local copies, waits for them, and re-layouts: 3.25 us -> 0.81 us
    reshape x1 -> x0, local copies, waits for them, and re-layouts: 1.27 us -> none  [fused_body(): factor_ranks.reshape(-1)]
    slice x0 -> x1, local copies, waits for them, and re-layouts: none -> 1.06 us  [fused_body(): inner_mean, top_inverse = (rows[0, :, :1], rows[1, :, :1])]
    squeeze x0 -> x1, local copies, waits for them, and re-layouts: none -> 1.04 us  [fused_body(): lax.dynamic_index_in_dim(proj_weight, layer_order[0], 0, keepdims=False)]
    dynamic_slice x1 -> x0, local copies, waits for them, and re-layouts: 1.04 us -> none  [fused_body(): lax.dynamic_index_in_dim(proj_weight, layer_order[0], 0, keepdims=False)]
where the time goes in v2:
time: 78.5 us; the launch traced here: 78.3 us
  Pallas kernels  69 us (88%)
  other arithmetic  3.61 us (5%)
  local copies, waits for them, and re-layouts  2.91 us (4%)
  between operations  2.75 us (4%)
    pallas_call x1, Pallas kernels, fused_body(): pl.pallas_call(functools.partial(fused_kernel, n_z), out_shape=(jax.Shape...  69 us
    convert_element_type x1, other arithmetic, fused_body(): return (hidden_grad.astype(half), basis)  3.61 us

profile of v2, /device:TPU:0, one launch (start us, length us, event | category | flops | bytes accessed | tf_op | source)
XLA Modules:
  0.0 78.3 jit_solution(16108777676593374112)
XLA Ops:
  0.6 0.0 copy-start
  2.7 0.0 copy-done
  2.7 1.0 %dynamic-slice_bitcast_fusion.weight_ref = bf16[512,1024]{1,0:T(8,128)(2,1)} fusion(bf16[2,512,1024]{2,1,0:T(8,128)(2,1)S(1)} %copy-done, s32[]{:T(128)S(6)} %select_n.6), kind=kLoop, calls=%fused_computation.5 | loop fusion | bytes 2097156 | tf_op jit(solution)/shard_map/jit(dynamic_index_in_dim)/squeeze | solution.py:453
  3.8 69.0 %shard_map.86 = (f32[144,4096]{1,0:T(8,128)}, f32[2,144,128]{2,1,0:T(8,128)}, f32[2,512,128]{2,1,0:T(8,128)}) custom-call(s32[2,2]{1,0:T(2,128)} %ranks_ref.1, s32[2]{0:T(128)} %order_ref.1, bf16[2,144,4096]{2,1,0:T(8,128)(2,1)} %hidden_ref.1, bf16[2,144,1024]{2,1,0:T(8,128)(2,1)} %cot_ref.1, bf16[512,1024]{1,0:T(8,128)(2,1)} %dynamic-slice_bitcast_fusion.weight_ref, ...), custom_call_target="tpu_custom_call" | custom-call | tf_op jit(solution)/shard_map/pallas_call | solution.py:459
  72.8 1.1 %slice_reduce_fusion.1 = (f32[144]{0:T(256)S(1)}, f32[144]{0:T(256)S(1)}) fusion(f32[2,144,128]{2,1,0:T(8,128)} %get-tuple-element.5), kind=kLoop, calls=%fused_computation.7 | loop fusion | bytes 2304 | tf_op jit(solution)/shard_map/slice | solution.py:501
  73.8 0.0 copy-start.1
  73.9 3.6 %fusion.3 = bf16[144,4096]{1,0:T(8,128)(2,1)} fusion(f32[144,4096]{1,0:T(8,128)} %get-tuple-element.6, f32[144]{0:T(256)S(1)} %get-tuple-element.9, bf16[2,144,4096]{2,1,0:T(8,128)(2,1)} %hidden_ref.1, s32[]{:T(128)S(6)} %select_n.6, f32[144]{0:T(256)S(1)} %get-tuple-element.8), kind=kLoop, calls=%fused_computation.4 | loop fusion | flops 3538944 | bytes 4719748 | tf_op jit(solution)/shard_map/convert_element_type | solution.py:503
  77.5 0.0 copy-done.1
  77.5 0.8 %copy.10 = f32[2,512,128]{2,1,0:T(8,128)} copy(f32[2,512,128]{2,1,0:T(8,128)S(1)} %copy-done.1) | data formatting | bytes 1048576
Async XLA Ops:
  0.6 2.1 %copy-start = (bf16[2,512,1024]{2,1,0:T(8,128)(2,1)S(1)}, bf16[2,512,1024]{2,1,0:T(8,128)(2,1)}, u32[]{:S(2)}) copy-start(bf16[2,512,1024]{2,1,0:T(8,128)(2,1)} %param.9) | copy-start | bytes 6291460
  73.8 3.6 %copy-start.1 = (f32[2,512,128]{2,1,0:T(8,128)S(1)}, f32[2,512,128]{2,1,0:T(8,128)}, u32[]{:S(2)}) copy-start(f32[2,512,128]{2,1,0:T(8,128)} %get-tuple-element.13) | copy-start | bytes 1572868

commit v3 on v2

--- a/solution.py
+++ b/solution.py
@@ -317,6 +317,7 @@
         keep2[h] = acc[h, a, b] + s1_recv[h, b].astype(jnp.float32)
     in_plane(0)
     along_z(1)
+    in_plane(1)
     for h in range(2):
         arrived(s2_recv.at[h], recv_sem.at[4 + h])
         summed = keep2[h] + s2_recv[h].astype(jnp.float32)
@@ -363,8 +364,8 @@
     def _():
         to_sibling.start()
 
-    in_plane(1)
     in_plane(2)
+    relay(0)
     own_copy.wait()
     inner = gradient_columns(z, sib_sem.at[0], jnp.zeros((tokens, 1), jnp.float32))
 
@@ -398,10 +399,7 @@
         matrix = matrix - factor * (pivot_row * scale)
         unit = unit - factor * (unit_row * scale)
         if j == 20:
-            relay(0)
-        if j == 40:
             relay(1)
-    last_leg(0)
     pivots = jnp.where(on_diagonal, matrix, 0.0)
     left_pivot = jnp.sum(jnp.where(left, pivots, 0.0), axis=1, keepdims=True)
     right_pivot = jnp.sum(jnp.where(left, 0.0, pivots), axis=1, keepdims=True)
@@ -409,6 +407,8 @@
     send(l_send, l_recv, send_sem.at[20], recv_sem.at[20], sibling)
     arrived(l_recv, recv_sem.at[20])
 
+    relay(2)
+    last_leg(0)
     for i in range(2):
         for s in range(2):
             arrived(f_all.at[s, i], f_sem.at[s, i])
@@ -426,7 +426,6 @@
                 basis_ref[s, at : at + 128, :] = turned.T
 
     inner = gradient_columns(source_of(0), sib_sem.at[1], inner)
-    relay(2)
     last_leg(1)
     inner = gradient_columns(source_of(1), sib_sem.at[2], inner)
     last_leg(2)
@@ -494,7 +493,7 @@
             dma,
         ],
         compiler_params=pltpu.CompilerParams(
-            collective_id=0, has_side_effects=True, vmem_limit_bytes=60 * 1024 * 1024
+            collective_id=0, has_side_effects=True, vmem_limit_bytes=30 * 1024 * 1024
         ),
     )(factor_ranks, layer_order, hidden, cotangent, top_weight, norm_gain, prev_factor)
     top_hidden = lax.dynamic_index_in_dim(hidden, layer_order[0], 0, keepdims=False).astype(full)

time: 78.5 us -> 69.2 us (0.88)
  Pallas kernels: 69 us -> 58.7 us
  local copies, waits for them, and re-layouts: 2.91 us -> 5.73 us
  other arithmetic: 3.61 us -> 1.6 us
    pallas_call x1, Pallas kernels: 69 us -> 58.7 us  [fused_body(): pl.pallas_call(functools.partial(fused_kernel, n_z), out_shape=(jax.Shape...]
    unnamed x5 -> x15, local copies, waits for them, and re-layouts: 0.81 us -> 5.51 us
    convert_element_type x1, other arithmetic: 3.61 us -> 1.6 us  [fused_body(): return (hidden_grad.astype(half), basis)]
    squeeze x1, local copies, waits for them, and re-layouts: 1.04 us -> 0.08 us  [fused_body(): lax.dynamic_index_in_dim(proj_weight, layer_order[0], 0, keepdims=False)]
    slice x1, local copies, waits for them, and re-layouts: 1.06 us -> 0.14 us  [fused_body(): inner_mean, top_inverse = (rows[0, :, :1], rows[1, :, :1])]
where the time goes in v3:
time: 69.2 us; the launch traced here: 68.8 us
  Pallas kernels  58.7 us (85%)
  local copies, waits for them, and re-layouts  5.73 us (8%)
  between operations  2.79 us (4%)
  other arithmetic  1.6 us (2%)
    pallas_call x1, Pallas kernels, fused_body(): pl.pallas_call(functools.partial(fused_kernel, n_z), out_shape=(jax.Shape...  58.7 us
    unnamed x15, local copies, waits for them, and re-layouts  5.51 us
    convert_element_type x1, other arithmetic, fused_body(): return (hidden_grad.astype(half), basis)  1.6 us

profile of v3, /device:TPU:0, one launch (start us, length us, event | category | flops | bytes accessed | tf_op | source)
XLA Modules:
  0.0 68.8 jit_solution(2935732557772904446)
XLA Ops:
  0.6 0.0 copy-start
  0.6 0.0 copy-start.2
  2.8 0.0 copy-done
  2.8 0.1 dynamic-slice_bitcast_fusion.weight_ref
  2.9 0.0 copy-done.2
  2.9 0.0 copy-start.1
  2.9 1.7 %copy-done.1 = bf16[2,144,4096]{2,1,0:T(8,128)(2,1)S(1)} copy-done((bf16[2,144,4096]{2,1,0:T(8,128)(2,1)S(1)}, bf16[2,144,4096]{2,1,0:T(8,128)(2,1)}, u32[]{:S(2)}) %copy-start.1) | copy-done | bytes 2359320
  4.5 0.0 copy-start.3
  4.5 0.9 %copy-done.3 = bf16[2,512,128]{2,1,0:T(8,128)(2,1)S(1)} copy-done((bf16[2,512,128]{2,1,0:T(8,128)(2,1)S(1)}, bf16[2,512,128]{2,1,0:T(8,128)(2,1)}, u32[]{:S(2)}) %copy-start.3) | copy-done | bytes 262168
  5.5 0.0 copy-start.4
  5.5 0.8 %copy-done.4 = f32[2,4096]{1,0:T(2,128)S(1)} copy-done((f32[2,4096]{1,0:T(2,128)S(1)}, f32[2,4096]{1,0:T(2,128)}, u32[]{:S(2)}) %copy-start.4) | copy-done | bytes 32792
  6.2 0.0 copy-start.5
  6.2 0.7 copy-done.5
  6.9 0.0 copy-start.6
  6.9 0.7 copy-done.6
  7.6 58.7 %shard_map.86 = (f32[144,4096]{1,0:T(8,128)S(1)}, f32[2,144,128]{2,1,0:T(8,128)S(1)}, f32[2,512,128]{2,1,0:T(8,128)S(1)}) custom-call(s32[2,2]{1,0:T(2,128)S(1)} %copy-done.6, s32[2]{0:T(128)S(1)} %copy-done.5, bf16[2,144,4096]{2,1,0:T(8,128)(2,1)S(1)} %copy-done.1, bf16[2,144,1024]{2,1,0:T(8,128)(2,1)S(1)} %copy-done.2, ...), custom_call_target="tpu_custom_call" | custom-call | tf_op jit(solution)/shard_map/pallas_call | solution.py:458
  66.3 0.1 slice_reduce_fusion.1
  66.5 1.6 %fusion.3 = bf16[144,4096]{1,0:T(8,128)(2,1)} fusion(f32[144,4096]{1,0:T(8,128)S(1)} %get-tuple-element.6, f32[144]{0:T(256)S(1)} %get-tuple-element.9, bf16[2,144,4096]{2,1,0:T(8,128)(2,1)S(1)} %copy-done.1, s32[]{:T(128)S(6)} %select_n.6, f32[144]{0:T(256)S(1)} %get-tuple-element.8), kind=kLoop, calls=%fused_computation.4 | loop fusion | flops 3538944 | bytes 4719748 | tf_op jit(solution)/shard_map/convert_element_type | solution.py:502
  68.1 0.8 %copy.10 = f32[2,512,128]{2,1,0:T(8,128)} copy(f32[2,512,128]{2,1,0:T(8,128)S(1)} %get-tuple-element.13) | data formatting | bytes 1048576
Async XLA Ops:
  0.6 2.1 %copy-start = (bf16[2,512,1024]{2,1,0:T(8,128)(2,1)S(1)}, bf16[2,512,1024]{2,1,0:T(8,128)(2,1)}, u32[]{:S(2)}) copy-start(bf16[2,512,1024]{2,1,0:T(8,128)(2,1)} %param.9) | copy-start | bytes 6291460
  0.6 2.2 %copy-start.2 = (bf16[2,144,1024]{2,1,0:T(8,128)(2,1)S(1)}, bf16[2,144,1024]{2,1,0:T(8,128)(2,1)}, u32[]{:S(2)}) copy-start(bf16[2,144,1024]{2,1,0:T(8,128)(2,1)} %cot_ref.1) | copy-start | bytes 1769476
  2.9 1.7 %copy-start.1 = (bf16[2,144,4096]{2,1,0:T(8,128)(2,1)S(1)}, bf16[2,144,4096]{2,1,0:T(8,128)(2,1)}, u32[]{:S(2)}) copy-start(bf16[2,144,4096]{2,1,0:T(8,128)(2,1)} %hidden_ref.1) | copy-start | bytes 7077892
  4.5 0.9 %copy-start.3 = (bf16[2,512,128]{2,1,0:T(8,128)(2,1)S(1)}, bf16[2,512,128]{2,1,0:T(8,128)(2,1)}, u32[]{:S(2)}) copy-start(bf16[2,512,128]{2,1,0:T(8,128)(2,1)} %factor_ref.1) | copy-start | bytes 786436
  5.5 0.8 %copy-start.4 = (f32[2,4096]{1,0:T(2,128)S(1)}, f32[2,4096]{1,0:T(2,128)}, u32[]{:S(2)}) copy-start(f32[2,4096]{1,0:T(2,128)} %gain_ref.1) | copy-start | bytes 98308
  6.2 0.7 copy-start.5
  6.9 0.7 copy-start.6

commit v4 on v3

--- a/solution.py
+++ b/solution.py
@@ -117,9 +117,9 @@
 
 def fused_kernel(
     n_z, ranks_ref, order_ref, hidden_ref, cot_ref, weight_ref, gain_ref, factor_ref,
-    scaled_ref, rows_ref, basis_ref,
+    grad_ref, basis_ref,
     acc, s0_send, s0_recv, s1_send, s1_recv, s2_send, s2_recv, keep2, s3_send, s3_recv,
-    f_send, f_all, g_all, z_send, z_all, l_send, l_recv, w_all, inverse,
+    f_send, f_all, g_all, z_send, z_all, l_send, l_recv, w_all, scaled, inverse,
     send_sem, recv_sem, f_sem, w_send, w_recv, sib_sem, own_sem,
 ):
     q = lax.axis_index("dp")
@@ -248,7 +248,7 @@
                 preferred_element_type=jnp.float32,
             )
             product = product * gain_ref[pl.ds(top, 1), pl.ds(at, own_rows)]
-            scaled_ref[:, pl.ds(at, own_rows)] = product
+            scaled[:, pl.ds(at, own_rows)] = product
             unit_rows = hidden_ref[top, :, pl.ds(at, own_rows)].astype(jnp.float32) * inverse[top]
             inner = inner + jnp.sum(product * unit_rows, axis=1, keepdims=True)
         return inner
@@ -430,8 +430,17 @@
     inner = gradient_columns(source_of(1), sib_sem.at[2], inner)
     last_leg(2)
     inner = gradient_columns(source_of(2), sib_sem.at[3], inner)
-    rows_ref[0] = jnp.broadcast_to(inner / width, (tokens, 128))
-    rows_ref[1] = jnp.broadcast_to(inverse[top], (tokens, 128))
+    inner_mean = inner / width
+
+    def finish(step, carry):
+        at = pl.multiple_of(step * own_rows, own_rows)
+        unit_rows = hidden_ref[top, :, pl.ds(at, own_rows)].astype(jnp.float32) * inverse[top]
+        grad_ref[:, pl.ds(at, own_rows)] = (
+            inverse[top] * (scaled[:, pl.ds(at, own_rows)] - unit_rows * inner_mean)
+        ).astype(jnp.bfloat16)
+        return carry
+
+    lax.fori_loop(0, width // own_rows, finish, 0)
 
     for copy in pending:
         copy.wait_send()
@@ -455,15 +464,14 @@
     half = jnp.bfloat16
     full = jnp.float32
     dma = pltpu.SemaphoreType.DMA
-    scaled, rows, basis = pl.pallas_call(
+    return pl.pallas_call(
         functools.partial(fused_kernel, n_z),
         out_shape=(
-            jax.ShapeDtypeStruct((tokens, width), full),
-            jax.ShapeDtypeStruct((2, tokens, 128), full),
+            jax.ShapeDtypeStruct((tokens, width), half),
             jax.ShapeDtypeStruct((layers, owned, prev_factor.shape[2]), full),
         ),
         in_specs=[smem, smem] + [vmem] * 5,
-        out_specs=(vmem, vmem, vmem),
+        out_specs=(vmem, vmem),
         scratch_shapes=[
             pltpu.VMEM((2, 2, 2, n_z, 128, 128), full),
             pltpu.VMEM((2, 2, 2, n_z, 128, 128), half),
@@ -483,6 +491,7 @@
             pltpu.VMEM((64, 128), full),
             pltpu.VMEM((64, 128), full),
             pltpu.VMEM((width, kv), half),
+            pltpu.VMEM((tokens, width), full),
             pltpu.VMEM((2, tokens, 1), full),
             dma((24,)),
             dma((24,)),
@@ -496,10 +505,6 @@
             collective_id=0, has_side_effects=True, vmem_limit_bytes=30 * 1024 * 1024
         ),
     )(factor_ranks, layer_order, hidden, cotangent, top_weight, norm_gain, prev_factor)
-    top_hidden = lax.dynamic_index_in_dim(hidden, layer_order[0], 0, keepdims=False).astype(full)
-    inner_mean, top_inverse = rows[0, :, :1], rows[1, :, :1]
-    hidden_grad = top_inverse * (scaled - top_hidden * top_inverse * inner_mean)
-    return (hidden_grad.astype(half), basis)
 
 
 def solution(mesh):

time: 69.2 us -> 66.5 us (0.961)
  local copies, waits for them, and re-layouts: 5.73 us -> 3.57 us
  other arithmetic: 1.6 us -> 0 us
  Pallas kernels: 58.7 us -> 59.8 us
    unnamed x15 -> x16, local copies, waits for them, and re-layouts: 5.51 us -> 3.5 us
    convert_element_type x1 -> x0, other arithmetic: 1.6 us -> none  [fused_body(): return (hidden_grad.astype(half), basis)]
    pallas_call x1, Pallas kernels: 58.7 us -> 59.8 us  [fused_body(): pl.pallas_call(functools.partial(fused_kernel, n_z), out_shape=(jax.Shape...]
where the time goes in v4:
time: 66.5 us; the launch traced here: 66.3 us
  Pallas kernels  59.8 us (90%)
  local copies, waits for them, and re-layouts  3.57 us (5%)
  between operations  2.94 us (4%)
    pallas_call x1, Pallas kernels, fused_body(): pl.pallas_call(functools.partial(fused_kernel, n_z), out_shape=(jax.Shape...  59.8 us
    unnamed x16, local copies, waits for them, and re-layouts  3.5 us

profile of v4, /device:TPU:0, one launch (start us, length us, event | category | flops | bytes accessed | tf_op | source)
XLA Modules:
  0.0 66.3 jit_solution(9090395890207161902)
XLA Ops:
  0.6 0.0 copy-start
  0.6 0.0 copy-start.5
  0.7 0.0 copy-start.6
  0.7 0.0 copy-start.3
  0.7 0.0 copy-start.4
  0.7 0.0 copy-start.2
  2.9 0.0 copy-done
  2.9 0.1 dynamic-slice_bitcast_fusion.weight_ref
  3.0 0.0 copy-done.5
  3.0 0.0 copy-done.6
  3.0 0.0 copy-done.3
  3.0 0.0 copy-done.4
  3.0 0.0 copy-done.2
  3.0 0.0 copy-start.1
  3.0 1.7 %copy-done.1 = bf16[2,144,4096]{2,1,0:T(8,128)(2,1)S(1)} copy-done((bf16[2,144,4096]{2,1,0:T(8,128)(2,1)S(1)}, bf16[2,144,4096]{2,1,0:T(8,128)(2,1)}, u32[]{:S(2)}) %copy-start.1) | copy-done | bytes 2359320
  4.7 59.8 %shard_map.86 = (bf16[144,4096]{1,0:T(8,128)(2,1)S(1)}, f32[2,512,128]{2,1,0:T(8,128)S(1)}) custom-call(s32[2,2]{1,0:T(2,128)S(1)} %copy-done.6, s32[2]{0:T(128)S(1)} %copy-done.5, bf16[2,144,4096]{2,1,0:T(8,128)(2,1)S(1)} %copy-done.1, bf16[2,144,1024]{2,1,0:T(8,128)(2,1)S(1)} %copy-done.2, bf16[512,1024]{1,0:T(8,128)(2,1)S(1)} %dynamic-slice_bitcast_fusion.weight_ref, ...), custom_call_target="tpu_custom_call" | custom-call | tf_op jit(solution)/shard_map/pallas_call | solution.py:467
  64.5 1.0 %copy.11 = bf16[144,4096]{1,0:T(8,128)(2,1)} copy(bf16[144,4096]{1,0:T(8,128)(2,1)S(1)} %get-tuple-element.4) | data formatting | bytes 2359296
  65.5 0.8 %copy.12 = f32[2,512,128]{2,1,0:T(8,128)} copy(f32[2,512,128]{2,1,0:T(8,128)S(1)} %get-tuple-element.5) | data formatting | bytes 1048576
Async XLA Ops:
  0.6 2.3 %copy-start = (bf16[2,512,1024]{2,1,0:T(8,128)(2,1)S(1)}, bf16[2,512,1024]{2,1,0:T(8,128)(2,1)}, u32[]{:S(2)}) copy-start(bf16[2,512,1024]{2,1,0:T(8,128)(2,1)} %param.9) | copy-start | bytes 6291460
  0.6 2.3 %copy-start.5 = (s32[2]{0:T(128)S(1)}, s32[2]{0:T(128)}, u32[]{:S(2)}) copy-start(s32[2]{0:T(128)} %order_ref.1) | copy-start | bytes 28
  0.7 2.3 %copy-start.6 = (s32[2,2]{1,0:T(2,128)S(1)}, s32[2,2]{1,0:T(2,128)}, u32[]{:S(2)}) copy-start(s32[2,2]{1,0:T(2,128)} %ranks_ref.1) | copy-start | bytes 52
  0.7 2.3 %copy-start.3 = (bf16[2,512,128]{2,1,0:T(8,128)(2,1)S(1)}, bf16[2,512,128]{2,1,0:T(8,128)(2,1)}, u32[]{:S(2)}) copy-start(bf16[2,512,128]{2,1,0:T(8,128)(2,1)} %factor_ref.1) | copy-start | bytes 786436
  0.7 2.3 %copy-start.4 = (f32[2,4096]{1,0:T(2,128)S(1)}, f32[2,4096]{1,0:T(2,128)}, u32[]{:S(2)}) copy-start(f32[2,4096]{1,0:T(2,128)} %gain_ref.1) | copy-start | bytes 98308
  0.7 2.3 %copy-start.2 = (bf16[2,144,1024]{2,1,0:T(8,128)(2,1)S(1)}, bf16[2,144,1024]{2,1,0:T(8,128)(2,1)}, u32[]{:S(2)}) copy-start(bf16[2,144,1024]{2,1,0:T(8,128)(2,1)} %cot_ref.1) | copy-start | bytes 1769476
  3.0 1.7 %copy-start.1 = (bf16[2,144,4096]{2,1,0:T(8,128)(2,1)S(1)}, bf16[2,144,4096]{2,1,0:T(8,128)(2,1)}, u32[]{:S(2)}) copy-start(bf16[2,144,4096]{2,1,0:T(8,128)(2,1)} %hidden_ref.1) | copy-start | bytes 7077892
